TPU v7x, 32 devices: a whole 2x2x4 slice. The times are simulated.
32 devices in a mesh: group: 2 (over y), ctx: 4 (over z), head: 2 (over x), req: 2 (over core).
Axes of the slice: x: 2, y: 2, z: 4, core: 2. Of those that a mesh axis runs over, the one named last changes fastest.
Arguments:
- kda_query: bfloat16 [4, 768, 4096], P(('group', 'req'), 'ctx', 'head'), parts along dimension 0, may hold values from -6 to 6
- kda_key: bfloat16 [4, 768, 4096], P(('group', 'req'), 'ctx', 'head'), parts along dimension 0, may hold values from -6 to 6
- kda_value: bfloat16 [4, 768, 4096], P(('group', 'req'), 'ctx', 'head'), parts along dimension 0, may hold values from -6 to 6
- log_decay: bfloat16 [4, 768, 4096], P(('group', 'req'), 'ctx', 'head'), parts along dimension 0, may hold values from -1 to 0
- write_strength: float32 [4, 32, 768], P(('group', 'req'), 'head', 'ctx'), parts along dimension 0, may hold values from 0.1 to 0.95
- mla_query: bfloat16 [4, 768, 18432], P(('group', 'req'), 'ctx', 'head'), parts along dimension 0, may hold values from -18 to 18
- latents: bfloat16 [4, 768, 576], P(('group', 'req'), 'ctx'), parts along dimension 0, may hold values from -8 to 8
- value_up: bfloat16 [32, 512, 128], P('head'), may hold values from -0.25 to 0.25
- out_proj: bfloat16 [4096, 2304], P('head'), may hold values from -0.09375 to 0.09375
- doc_lengths: int32 [4, 8], P(('group', 'req')), parts along dimension 0, may hold values from 1 to 288, 768 in all within a row
Outputs:
- kda_out: bfloat16 [4, 768, 4096], P(('group', 'req'), 'ctx', 'head'), parts along dimension 0
- mixed: bfloat16 [4, 768, 2304], P(('group', 'req'), ('ctx', 'head')), parts along dimension 0
There are 2 independent parts, one for each index of `group`. A program takes and returns all parts, laid end to end along the dimension named above; an argument that names none is the same for every part. Nothing has to cross between parts.
Inputs may be any that keep to these rules, and one draw needn't show every extreme that they name: `doc_lengths`: each row's lengths sum to 768, and each row's longest prompt has exactly 288 positions.
All inputs are finite; a program needn't handle non-finite values.
Results may differ from a plain program's by a relative error of at most 0.009.
Values may be sent and summed in bfloat16 or wider, within the bound.
A program may use at most 128 MiB of HBM per device.

v0:
```python
import math
import jax
import jax.numpy as jnp
from jax import lax
from jax.sharding import PartitionSpec as P

ROPE = 64
NOPE = 128
SPAN = 64
top_value = lax.Precision.HIGHEST
masked_score = -1e30


def from_behind(value, axis, by):
    peers = lax.axis_size(axis)
    pairs = [(i, i + by) for i in range(peers) if 0 <= i + by < peers]
    return lax.ppermute(value, axis, pairs)


def unit_length(values):
    return values * lax.rsqrt(jnp.sum(values * values, axis=-1, keepdims=True) + 1e-06)


def doc_index(position_list, doc_ends):
    return jnp.sum((doc_ends[None, :] <= position_list[:, None]).astype(jnp.int32), axis=1)


def span_terms(query_rows, key_rows, value_rows, decay_rows, strength, doc_ids, prev_doc):
    span_len = key_rows.shape[1]
    state_dim = key_rows.shape[2]
    row_index = jnp.arange(span_len, dtype=jnp.int32)
    inclusive = (row_index[:, None] >= row_index[None, :]).astype(jnp.float32)
    summed = jnp.einsum("ij,hjc->hic", inclusive, decay_rows, precision=top_value)
    growth = jnp.exp(summed)
    key_hat = key_rows * growth
    key_tilde = key_rows * jnp.exp(-summed)
    query_estimate = query_rows * growth
    same_doc = doc_ids[:, None] == doc_ids[None, :]
    strict = same_doc & (row_index[:, None] > row_index[None, :])
    up_to = same_doc & (row_index[:, None] >= row_index[None, :])
    carried = (doc_ids == prev_doc).astype(jnp.float32)
    inner = jnp.einsum("hic,hjc->hij", key_hat, key_tilde, precision=top_value)
    lower_part = jnp.where(strict[None], inner * strength[:, :, None], 0.0)
    system = lower_part + jnp.eye(span_len, dtype=jnp.float32)[None]
    right_side = jnp.concatenate(
        [(strength * carried[None])[:, :, None] * key_hat, strength[:, :, None] * value_rows],
        axis=2,
    )
    solved = lax.linalg.triangular_solve(
        system, right_side, left_side=True, lower=True, unit_diagonal=True
    )
    weighted_key_rows = solved[:, :, :state_dim]
    update_rows = solved[:, :, state_dim:]
    attend = jnp.where(
        up_to[None], jnp.einsum("hic,hjc->hij", query_estimate, key_tilde, precision=top_value), 0.0
    )
    tail_mask = same_doc[span_len - 1].astype(jnp.float32)
    key_decay = key_rows * jnp.exp(summed[:, span_len - 1 :, :] - summed) * tail_mask[None, :, None]
    diagonal = (
        carried[span_len - 1]
        * growth[:, span_len - 1, :, None]
        * jnp.eye(state_dim, dtype=jnp.float32)[None]
    )
    transition = diagonal - jnp.einsum(
        "hjc,hjd->hcd", key_decay, weighted_key_rows, precision=top_value
    )
    offset = jnp.einsum("hjc,hjv->hcv", key_decay, update_rows, precision=top_value)
    return (query_estimate, carried, weighted_key_rows, update_rows, attend, transition, offset)


def span_output(terms, inbound_state):
    query_estimate, carried, weighted_key_rows, update_rows, attend, transition, offset = terms
    adjusted_rows = update_rows - jnp.einsum(
        "izy,iyn->izn", weighted_key_rows, inbound_state, precision=top_value
    )
    state_contribution = jnp.einsum(
        "izy,iyn->izn", query_estimate, inbound_state, precision=top_value
    )
    return carried[None, :, None] * state_contribution + jnp.einsum(
        "hij,hjv->hiv", attend, adjusted_rows, precision=top_value
    )


def apply_map(transition, offset, inbound_state):
    return jnp.einsum("hcd,hdv->hcv", transition, inbound_state, precision=top_value) + offset


def local(
    kda_query,
    kda_key,
    kda_value,
    log_decay,
    write_strength,
    mla_query,
    latents,
    value_up,
    out_proj,
    doc_lengths,
):
    tokens_dev = kda_query.shape[1]
    heads_dev = write_strength.shape[1]
    state_dim = kda_query.shape[2] // heads_dev
    ctx_count = lax.axis_size("ctx")
    ctx_place = lax.axis_index("ctx")
    first_pos = ctx_place * tokens_dev
    positions = first_pos + jnp.arange(tokens_dev, dtype=jnp.int32)
    doc_ends = jnp.cumsum(doc_lengths[0])
    doc_ids = doc_index(positions, doc_ends)

    def head_first(packed):
        return jnp.transpose(
            packed[0].astype(jnp.float32).reshape(tokens_dev, heads_dev, state_dim), (1, 0, 2)
        )

    query_rows = unit_length(head_first(kda_query))
    key_rows = unit_length(head_first(kda_key))
    value_rows = head_first(kda_value)
    decay_rows = head_first(log_decay)
    strength = write_strength[0]
    span_list = []
    eye_batch = jnp.broadcast_to(
        jnp.eye(state_dim, dtype=jnp.float32), (heads_dev, state_dim, state_dim)
    )
    transition = eye_batch
    offset = jnp.zeros((heads_dev, state_dim, state_dim), jnp.float32)
    for span_begin in range(0, tokens_dev, SPAN):
        span_stop = span_begin + SPAN
        prev_doc = doc_index(positions[span_begin : span_begin + 1] - 1, doc_ends)[0]
        terms = span_terms(
            query_rows[:, span_begin:span_stop],
            key_rows[:, span_begin:span_stop],
            value_rows[:, span_begin:span_stop],
            decay_rows[:, span_begin:span_stop],
            strength[:, span_begin:span_stop],
            doc_ids[span_begin:span_stop],
            prev_doc,
        )
        span_list.append(terms)
        offset = apply_map(terms[5], terms[6], offset)
        transition = jnp.einsum("hcd,hde->hce", terms[5], transition, precision=top_value)

    def relay(turn_index, inbound_state):
        outgoing = apply_map(transition, offset, inbound_state)
        return from_behind(outgoing.astype(jnp.bfloat16), "ctx", 1).astype(outgoing.dtype)

    inbound_state = lax.fori_loop(0, ctx_count - 1, relay, jnp.zeros_like(offset))
    pieces = []
    state_now = inbound_state
    for span_number, terms in enumerate(span_list):
        pieces.append(span_output(terms, state_now))
        if span_number + 1 < len(span_list):
            state_now = apply_map(terms[5], terms[6], state_now)
    kda_out = (
        jnp.transpose(jnp.concatenate(pieces, axis=1), (1, 0, 2))
        .reshape(1, tokens_dev, heads_dev * state_dim)
        .astype(jnp.bfloat16)
    )
    width = latents.shape[2]
    lat_dim = value_up.shape[1]
    score_scale = 1.0 / math.sqrt(NOPE + ROPE)
    query_flat = mla_query[0].reshape(tokens_dev * heads_dev, width)
    row_pos = jnp.repeat(positions, heads_dev)
    row_doc = jnp.repeat(doc_ids, heads_dev)
    row_total_count = tokens_dev * heads_dev
    row_peak = jnp.full((row_total_count,), masked_score, jnp.float32)
    block_rows = lax.all_gather(latents, "ctx", axis=1, tiled=True)[0]
    row_count = block_rows.shape[0]
    key_pos = jnp.arange(row_count, dtype=jnp.int32)
    key_doc = doc_index(key_pos, doc_ends)
    scores = (
        lax.dot_general(
            query_flat, block_rows, (((1,), (1,)), ((), ())), preferred_element_type=jnp.float32
        )
        * score_scale
    )
    allowed = (
        (key_pos[None, :] <= row_pos[:, None])
        & (key_pos[None, :] >= 0)
        & (key_doc[None, :] == row_doc[:, None])
    )
    new_peak = jnp.maximum(row_peak, jnp.max(jnp.where(allowed, scores, masked_score), axis=1))
    exponent = jnp.where(allowed, jnp.exp(scores - new_peak[:, None]), 0.0)
    row_total = jnp.sum(exponent, axis=1)
    weighted = jnp.dot(
        exponent.astype(jnp.bfloat16), block_rows[:, :lat_dim], preferred_element_type=jnp.float32
    )
    row_peak, row_total, weighted = (new_peak, row_total, weighted)
    context = (
        (weighted / row_total[:, None]).astype(jnp.bfloat16).reshape(tokens_dev, heads_dev, lat_dim)
    )
    head_out = jnp.einsum(
        "thl,hlv->thv", context, value_up, preferred_element_type=jnp.float32
    ).astype(jnp.bfloat16)
    head_out = head_out.reshape(tokens_dev, heads_dev * value_up.shape[2])
    mixed = lax.psum_scatter(
        jnp.dot(head_out, out_proj, preferred_element_type=jnp.float32).astype(jnp.bfloat16),
        "head",
        scatter_dimension=0,
        tiled=True,
    )
    return (kda_out, mixed[None])


def solution(mesh):
    placed = (
        P(("group", "req"), "ctx", "head"),
        P(("group", "req"), "ctx", "head"),
        P(("group", "req"), "ctx", "head"),
        P(("group", "req"), "ctx", "head"),
        P(("group", "req"), "head", "ctx"),
        P(("group", "req"), "ctx", "head"),
        P(("group", "req"), "ctx", None),
        P("head", None, None),
        P("head", None),
        P(("group", "req"), None),
    )
    return jax.shard_map(
        local,
        mesh=mesh,
        in_specs=placed,
        out_specs=(P(("group", "req"), "ctx", "head"), P(("group", "req"), ("ctx", "head"), None)),
        check_vma=False,
    )
```

profile of v0, /device:TPU:0, one launch (start us, length us, event | category | flops | bytes accessed | tf_op | source)
XLA Modules:
  0.0 443.5 jit_solution(2530594987979370844)
XLA Ops:
  8.8 23.7 %all_gather.3 = bf16[1,768,576]{2,1,0:T(8,128)(2,1)S(1)} all-gather(bf16[1,192,576]{2,1,0:T(8,128)(2,1)} %param.20), channel_id=1, replica_groups=mesh['group'=2,'ctx'=4,'head'=2,'req'=2] {'ctx'}, dimensions={1}, use_global_device_ids=true | all-gather | bytes 1105920 | tf_op jit(solution)/shard_map/all_gather | solution.py:166
  32.5 7.0 %reshape_squeeze.3 = bf16[3072,576]{1,0:T(8,128)(2,1)} reshape(bf16[1,192,9216]{2,1,0:T(8,128)(2,1)} %param.19) | data formatting | bytes 7077888 | tf_op jit(solution)/shard_map/reshape;squeeze | solution.py:161
  39.4 6.7 %select_reduce_fusion = (f32[3072]{0:T(1024)S(1)}, f32[3072,768]{0,1:T(8,128)S(1)}) fusion(s32[3072]{0:T(1024)S(1)} %eq.140, s32[3072]{0:T(1024)S(1)} %le.114, s32[768]{0:T(1024)S(1)} %convert_reduce_fusion, bf16[3072,576]{1,0:T(8,128)(2,1)} %reshape_squeeze.3, bf16[1,768,576]{2,1,0:T(8,128)(2,1)S(1)} %all_gather.3), kind=kOutput, calls=%fused_computation.7 | convolution fusion | flops 2732061696 | bytes 13900800 | tf_op jit(solution)/shard_map/dot_general | solution.py:171
  46.2 3.6 fusion.6
  49.8 4.3 divide_convert_fusion
  54.2 3.7 fusion.20
  57.9 3.0 convolution_convert_fusion
  65.9 2.0 compare_convert_fusion.2
  69.7 1.3 convert_bitcast_fusion.1
  73.3 1.9 fusion.30
  75.2 80.0 %custom-call.8 = f32[16,1,64,64]{2,3,1,0:T(8,128)} custom-call(f32[16,1,64,64]{3,2,1,0:T(8,128)} %fusion.30), custom_call_target="InvertDiagBlocksLowerTriangular" | custom-call | tf_op jit(solution)/shard_map/triangular_solve/custom-call.1 | solution.py:49
  155.2 1.3 convert_bitcast_fusion
  157.8 2.8 broadcast_multiply_fusion.2
  160.6 1.4 slice_multiply_fusion.4
  163.1 1.9 fusion.68
  165.1 1.3 slice_multiply_fusion.18
  166.3 2.1 convolution_subtract_fusion
  168.4 2.1 fusion.62
  170.5 2.0 convolution_add_fusion.5
  172.4 1.9 fusion.35
  174.3 80.2 %custom-call.7 = f32[16,1,64,64]{2,3,1,0:T(8,128)} custom-call(f32[16,1,64,64]{3,2,1,0:T(8,128)} %fusion.35), custom_call_target="InvertDiagBlocksLowerTriangular" | custom-call | tf_op jit(solution)/shard_map/triangular_solve/custom-call.1 | solution.py:49
  254.5 2.4 fusion.48
  256.9 2.9 fusion.66
  259.8 3.1 convolution_subtract_fusion.1
  262.9 1.9 fusion.40
  264.7 80.2 %custom-call.6 = f32[16,1,64,64]{2,3,1,0:T(8,128)} custom-call(f32[16,1,64,64]{3,2,1,0:T(8,128)} %fusion.40), custom_call_target="InvertDiagBlocksLowerTriangular" | custom-call | tf_op jit(solution)/shard_map/triangular_solve/custom-call.1 | solution.py:49
  344.9 1.4 slice_multiply_fusion.20
  346.4 3.1 convolution_add_fusion.4
  350.6 2.1 convolution_subtract_fusion.2
  352.7 1.1 fusion.119
  353.9 3.0 convolution_add_fusion.3
  356.8 1.1 fusion.117
  358.0 2.2 fusion.118
  360.2 53.5 %while.11 = (s32[]{:T(128)}, f32[16,128,128]{2,1,0:T(8,128)S(1)}, f32[16,128,128]{2,1,0:T(8,128)}, f32[16,128,128]{2,1,0:T(8,128)}, s32[]{:T(128)}, /*index=5*/s32[]{:T(128)}) while((s32[]{:T(128)}, f32[16,128,128]{2,1,0:T(8,128)S(1)}, f32[16,128,128]{2,1,0:T(8,128)}, f32[16,128,128]{2,1,0:T(8,128)}, s32[]{:T(128)}, ...), condition=%wide.region_8.10_spmd.clone, body=%wide.region_7.9_spmd.clone.sunk | while | flops 403701760 | bytes 7340151 | solution.py:146
  360.2 3.5 fusion.158
  363.7 2.8 collective-permute-start
  366.5 9.6 %collective-permute-done = bf16[16,128,128]{2,1,0:T(8,128)(2,1)} collective-permute-done((bf16[16,128,128]{2,1,0:T(8,128)(2,1)}, bf16[16,128,128]{2,1,0:T(8,128)(2,1)}, u32[]{:S(2)}, u32[]{:S(2)}) %collective-permute-start) | collective-permute-done | bytes 524320 | tf_op jit(solution)/shard_map/while/body/eval_jaxpr/ppermute | solution.py:17
  377.3 3.5 fusion.158
  380.8 5.2 %collective-permute-start = (bf16[16,128,128]{2,1,0:T(8,128)(2,1)}, bf16[16,128,128]{2,1,0:T(8,128)(2,1)}, u32[]{:S(2)}, u32[]{:S(2)}) collective-permute-start(bf16[16,128,128]{2,1,0:T(8,128)(2,1)} %fusion.158), channel_id=1, source_target_pairs={{0,4},{4,8},{8,12},{1,5},{5,9},{9,13},{2,6},{6,10},{10,14},{3,7},{... | collective-permute-start | bytes 1572872 | tf_op jit(solution)/shard_map/while/body/eval_jaxpr/ppermute | solution.py:17
  385.9 8.7 %collective-permute-done = bf16[16,128,128]{2,1,0:T(8,128)(2,1)} collective-permute-done((bf16[16,128,128]{2,1,0:T(8,128)(2,1)}, bf16[16,128,128]{2,1,0:T(8,128)(2,1)}, u32[]{:S(2)}, u32[]{:S(2)}) %collective-permute-start) | collective-permute-done | bytes 524320 | tf_op jit(solution)/shard_map/while/body/eval_jaxpr/ppermute | solution.py:17
  395.8 3.5 fusion.158
  399.3 5.2 %collective-permute-start = (bf16[16,128,128]{2,1,0:T(8,128)(2,1)}, bf16[16,128,128]{2,1,0:T(8,128)(2,1)}, u32[]{:S(2)}, u32[]{:S(2)}) collective-permute-start(bf16[16,128,128]{2,1,0:T(8,128)(2,1)} %fusion.158), channel_id=1, source_target_pairs={{0,4},{4,8},{8,12},{1,5},{5,9},{9,13},{2,6},{6,10},{10,14},{3,7},{... | collective-permute-start | bytes 1572872 | tf_op jit(solution)/shard_map/while/body/eval_jaxpr/ppermute | solution.py:17
  404.5 7.8 %collective-permute-done = bf16[16,128,128]{2,1,0:T(8,128)(2,1)} collective-permute-done((bf16[16,128,128]{2,1,0:T(8,128)(2,1)}, bf16[16,128,128]{2,1,0:T(8,128)(2,1)}, u32[]{:S(2)}, u32[]{:S(2)}) %collective-permute-start) | collective-permute-done | bytes 524320 | tf_op jit(solution)/shard_map/while/body/eval_jaxpr/ppermute | solution.py:17
  413.7 2.4 convolution_subtract_fusion.5
  416.2 1.2 convolution_add_fusion.2
  418.9 1.2 convolution_add_fusion.1
  432.6 1.4 copy.39
  434.0 2.1 convert_element_type.184
  (128 shorter events, 29.5 us)
Async XLA Ops:
  7.2 47.0 %copy-start = (bf16[16,512,128]{2,1,0:T(8,128)(2,1)S(1)}, bf16[16,512,128]{2,1,0:T(8,128)(2,1)}, u32[]{:S(2)}) copy-start(bf16[16,512,128]{2,1,0:T(8,128)(2,1)} %param.21) | copy-start | bytes 6291460
  7.2 428.9 %reduce-scatter.2.cloned.1.call-start = ((), (), s32[]{:S(2)}) async-start(), calls=%async_computation.1 | async-start | bytes 1327104 | tf_op jit(solution)/shard_map/reduce_scatter | solution.py:195
  46.2 11.7 %slice-start = ((s8[9437184]{0:T(1024)(128)(4,1)}), s8[4194304]{0:T(1024)(128)(4,1)S(1)}, s32[]{:S(2)}) async-start(s8[9437184]{0:T(1024)(128)(4,1)} %bitcast.155), calls=%async_computation.2 | async-start | bytes 8388608
  49.8 8.1 %slice-start.1 = ((s8[9437184]{0:T(1024)(128)(4,1)}), s8[4194304]{0:T(1024)(128)(4,1)S(1)}, s32[]{:S(2)}) async-start(s8[9437184]{0:T(1024)(128)(4,1)} %bitcast.155), calls=%async_computation.3 | async-start | bytes 8388608
  49.8 8.1 %slice-start.2 = ((s8[9437184]{0:T(1024)(128)(4,1)}), s8[1048576]{0:T(1024)(128)(4,1)S(1)}, s32[]{:S(2)}) async-start(s8[9437184]{0:T(1024)(128)(4,1)} %bitcast.155), calls=%async_computation.4 | async-start | bytes 2097152
  57.9 3.6 copy-start.24
  61.7 7.9 %copy-start.28 = (f32[1,16,192]{2,1,0:T(8,128)S(1)}, f32[1,16,192]{2,1,0:T(8,128)}, u32[]{:S(2)}) copy-start(f32[1,16,192]{2,1,0:T(8,128)} %param.18) | copy-start | bytes 36868
  62.0 1.3 copy-start.21
  72.0 1.2 copy-start.2
  156.7 1.0 copy-start.3
  160.6 1.5 copy-start.26
  163.1 5.3 %copy-start.15 = (f32[16,64,256]{2,1,0:T(8,128)}, f32[16,64,256]{2,1,0:T(8,128)S(1)}, u32[]{:S(2)}) copy-start(f32[16,64,256]{2,1,0:T(8,128)S(1)} %fusion.52) | copy-start | bytes 3145732
  165.0 5.4 %copy-start.12 = (f32[16,128,128]{2,1,0:T(8,128)}, f32[16,128,128]{2,1,0:T(8,128)S(1)}, u32[]{:S(2)}) copy-start(f32[16,128,128]{2,1,0:T(8,128)S(1)} %fusion.68) | copy-start | bytes 3145732
  168.4 4.0 copy-start.8
  256.9 6.0 %copy-start.16 = (f32[16,64,256]{2,1,0:T(8,128)}, f32[16,64,256]{2,1,0:T(8,128)S(1)}, u32[]{:S(2)}) copy-start(f32[16,64,256]{2,1,0:T(8,128)S(1)} %fusion.48) | copy-start | bytes 3145732
  259.8 3.1 copy-start.5
  346.3 3.2 copy-start.22
  346.3 3.2 copy-start.23
  346.4 3.2 copy-start.27
  349.5 1.1 copy-start.6
  350.6 3.2 copy-start.18
  353.8 3.0 copy-start.10
  353.8 3.0 copy-start.20
  363.7 12.4 %collective-permute-start = (bf16[16,128,128]{2,1,0:T(8,128)(2,1)}, bf16[16,128,128]{2,1,0:T(8,128)(2,1)}, u32[]{:S(2)}, u32[]{:S(2)}) collective-permute-start(bf16[16,128,128]{2,1,0:T(8,128)(2,1)} %fusion.158), channel_id=1, source_target_pairs={{0,4},{4,8},{8,12},{1,5},{5,9},{9,13},{2,6},{6,10},{10,14},{3,7},{... | collective-permute-start | bytes 1572872 | tf_op jit(solution)/shard_map/while/body/eval_jaxpr/ppermute | solution.py:17
  380.8 13.9 %collective-permute-start = (bf16[16,128,128]{2,1,0:T(8,128)(2,1)}, bf16[16,128,128]{2,1,0:T(8,128)(2,1)}, u32[]{:S(2)}, u32[]{:S(2)}) collective-permute-start(bf16[16,128,128]{2,1,0:T(8,128)(2,1)} %fusion.158), channel_id=1, source_target_pairs={{0,4},{4,8},{8,12},{1,5},{5,9},{9,13},{2,6},{6,10},{10,14},{3,7},{... | collective-permute-start | bytes 1572872 | tf_op jit(solution)/shard_map/while/body/eval_jaxpr/ppermute | solution.py:17
  399.3 13.0 %collective-permute-start = (bf16[16,128,128]{2,1,0:T(8,128)(2,1)}, bf16[16,128,128]{2,1,0:T(8,128)(2,1)}, u32[]{:S(2)}, u32[]{:S(2)}) collective-permute-start(bf16[16,128,128]{2,1,0:T(8,128)(2,1)} %fusion.158), channel_id=1, source_target_pairs={{0,4},{4,8},{8,12},{1,5},{5,9},{9,13},{2,6},{6,10},{10,14},{3,7},{... | collective-permute-start | bytes 1572872 | tf_op jit(solution)/shard_map/while/body/eval_jaxpr/ppermute | solution.py:17
  413.7 2.4 copy-start.9
  413.7 2.4 copy-start.13
  416.2 1.2 copy-start.17
  417.4 1.2 copy-start.11
  417.4 1.5 copy-start.14
  418.9 1.2 copy-start.25
  421.3 1.0 copy-start.4
  423.4 1.2 copy-start.19
  425.7 1.3 copy-start.7
  432.5 3.6 copy-start.1
Sparse Core Ops, SparseCore 0:
  61.1 18.3 reduce-scatter.1
where the time goes:
time: 449 us; the launch traced here: 443 us
  other arithmetic  261 us (58%)
  matrix products  84.7 us (19%)
  waiting for transfers between devices  26.2 us (6%)
  blocking collectives  23.7 us (5%)
  between operations  17.1 us (4%)
  local copies, waits for them, and re-layouts  16.8 us (4%)
  starting transfers between devices  13.2 us (3%)
    another operation x5, other arithmetic, span_terms(): lax.linalg.triangular_solve(system, right_side, left_side=True, lower=Tru...  240 us
    ppermute x3, waiting for transfers between devices, from_behind(): return lax.ppermute(value, axis, pairs)  26.2 us
    all_gather x1, blocking collectives, local(): block_rows = lax.all_gather(latents, 'ctx', axis=1, tiled=True)[0]  23.7 us
    dot_general x8, matrix products, apply_map(): jnp.einsum('hcd,hdv->hcv', transition, inbound_state, precision=top_value)  19.1 us
    ppermute x3, starting transfers between devices, from_behind(): return lax.ppermute(value, axis, pairs)  13.1 us
  transfers between devices with their start and end apart: 4, of which 3 were waited for; matrix products, arithmetic and copies ran while one was open for 75% of the time, Pallas kernels for 0%

commit v1 on v0

--- a/solution.py
+++ b/solution.py
@@ -163,7 +163,20 @@
     row_doc = jnp.repeat(doc_ids, heads_dev)
     row_total_count = tokens_dev * heads_dev
     row_peak = jnp.full((row_total_count,), masked_score, jnp.float32)
-    block_rows = lax.all_gather(latents, "ctx", axis=1, tiled=True)[0]
+
+    def derive_figure(row_data):
+        formed = jnp.concatenate(
+            lax.all_to_all(
+                jnp.stack(lax.axis_size("ctx") * [row_data]),
+                axis_name="ctx",
+                split_axis=0,
+                concat_axis=0,
+            ),
+            axis=1,
+        )
+        return formed
+
+    block_rows = derive_figure(latents)[0]
     row_count = block_rows.shape[0]
     key_pos = jnp.arange(row_count, dtype=jnp.int32)
     key_doc = doc_index(key_pos, doc_ends)

time: 449 us -> 463 us (1.031)
  blocking collectives: 23.7 us -> 0 us
  matrix products: 84.7 us -> 99 us
  waiting for transfers between devices: 26.2 us -> 35.5 us
  starting transfers between devices: 13.2 us -> 21.4 us
  local copies, waits for them, and re-layouts: 16.8 us -> 23.1 us
    all_gather x1 -> x0, blocking collectives: 23.7 us -> none  [local(): block_rows = lax.all_gather(latents, 'ctx', axis=1, tiled=True)[0]]
    reduce_scatter x1, waiting for transfers between devices: 0.01 us -> 7.89 us  [local(): lax.psum_scatter(jnp.dot(head_out, out_proj, preferred_element_type=jnp.f...]
    all_to_all x0 -> x1, starting transfers between devices: none -> 6.32 us  [derive_figure(): lax.all_to_all(jnp.stack(lax.axis_size('ctx') * [row_data]), axis_name='c...]
  transfers between devices with their start and end apart: 4 -> 5, of which waited for: 3 -> 4; matrix products, arithmetic and copies ran while one was open for 75% -> 77% of each run, Pallas kernels for 0% -> 0%
where the time goes in v1:
time: 463 us; the launch traced here: 458 us
  other arithmetic  261 us (56%)
  matrix products  99 us (21%)
  waiting for transfers between devices  35.5 us (8%)
  local copies, waits for them, and re-layouts  23.1 us (5%)
  starting transfers between devices  21.4 us (5%)
  between operations  17.5 us (4%)
    another operation x5, other arithmetic, span_terms(): lax.linalg.triangular_solve(system, right_side, left_side=True, lower=Tru...  241 us
    ppermute x3, waiting for transfers between devices, from_behind(): return lax.ppermute(value, axis, pairs)  27.6 us
    dot_general x8, matrix products, apply_map(): jnp.einsum('hcd,hdv->hcv', transition, inbound_state, precision=top_value)  21.5 us
    ppermute x3, starting transfers between devices, from_behind(): return lax.ppermute(value, axis, pairs)  15.1 us
  transfers between devices with their start and end apart: 5, of which 4 were waited for; matrix products, arithmetic and copies ran while one was open for 77% of the time, Pallas kernels for 0%

profile of v1, /device:TPU:0, one launch (start us, length us, event | category | flops | bytes accessed | tf_op | source)
XLA Modules:
  0.0 457.6 jit_solution(15465716919965113255)
XLA Ops:
  7.2 2.1 stack.2
  9.3 6.3 %all-to-all-start = ((bf16[4,1,192,576]{3,2,1,0:T(8,128)(2,1)}), bf16[4,1,192,576]{3,2,1,0:T(8,128)(2,1)}, u32[]{:S(2)}, u32[]{:S(2)}) async-start(bf16[4,1,192,576]{3,2,1,0:T(8,128)(2,1)} %stack.2), calls=%async_computation | async-start | bytes 1966080 | tf_op jit(solution)/shard_map/all_to_all | solution.py:169
  23.0 1.9 compare_convert_fusion.2
  30.9 1.8 fusion.30
  32.7 80.2 %custom-call.8 = f32[16,1,64,64]{2,3,1,0:T(8,128)} custom-call(f32[16,1,64,64]{3,2,1,0:T(8,128)} %fusion.30), custom_call_target="InvertDiagBlocksLowerTriangular" | custom-call | tf_op jit(solution)/shard_map/triangular_solve/custom-call.1 | solution.py:49
  116.2 2.7 broadcast_multiply_fusion.2
  121.5 1.9 fusion.68
  124.7 2.1 convolution_subtract_fusion
  126.8 2.0 fusion.62
  128.8 2.0 convolution_add_fusion.5
  130.7 1.9 fusion.35
  132.6 80.2 %custom-call.7 = f32[16,1,64,64]{2,3,1,0:T(8,128)} custom-call(f32[16,1,64,64]{3,2,1,0:T(8,128)} %fusion.35), custom_call_target="InvertDiagBlocksLowerTriangular" | custom-call | tf_op jit(solution)/shard_map/triangular_solve/custom-call.1 | solution.py:49
  212.9 2.5 fusion.48
  215.5 2.9 fusion.66
  218.4 3.0 convolution_subtract_fusion.1
  221.5 1.9 fusion.40
  223.4 80.5 %custom-call.6 = f32[16,1,64,64]{2,3,1,0:T(8,128)} custom-call(f32[16,1,64,64]{3,2,1,0:T(8,128)} %fusion.40), custom_call_target="InvertDiagBlocksLowerTriangular" | custom-call | tf_op jit(solution)/shard_map/triangular_solve/custom-call.1 | solution.py:49
  305.4 3.1 convolution_add_fusion.4
  310.0 2.1 convolution_subtract_fusion.2
  313.3 2.9 convolution_add_fusion.3
  317.3 2.1 fusion.116
  319.5 56.8 %while.11 = (s32[]{:T(128)}, f32[16,128,128]{2,1,0:T(8,128)S(1)}, f32[16,128,128]{2,1,0:T(8,128)}, f32[16,128,128]{2,1,0:T(8,128)}, s32[]{:T(128)}, /*index=5*/s32[]{:T(128)}) while((s32[]{:T(128)}, f32[16,128,128]{2,1,0:T(8,128)S(1)}, f32[16,128,128]{2,1,0:T(8,128)}, f32[16,128,128]{2,1,0:T(8,128)}, s32[]{:T(128)}, ...), condition=%wide.region_8.10_spmd.clone, body=%wide.region_7.9_spmd.clone.sunk | while | flops 403701760 | bytes 7340151 | solution.py:146
  319.5 3.5 fusion.157
  323.0 4.7 %collective-permute-start = (bf16[16,128,128]{2,1,0:T(8,128)(2,1)}, bf16[16,128,128]{2,1,0:T(8,128)(2,1)}, u32[]{:S(2)}, u32[]{:S(2)}) collective-permute-start(bf16[16,128,128]{2,1,0:T(8,128)(2,1)} %fusion.157), channel_id=1, source_target_pairs={{0,4},{4,8},{8,12},{1,5},{5,9},{9,13},{2,6},{6,10},{10,14},{3,7},{... | collective-permute-start | bytes 1572872 | tf_op jit(solution)/shard_map/while/body/eval_jaxpr/ppermute | solution.py:17
  327.7 10.1 %collective-permute-done = bf16[16,128,128]{2,1,0:T(8,128)(2,1)} collective-permute-done((bf16[16,128,128]{2,1,0:T(8,128)(2,1)}, bf16[16,128,128]{2,1,0:T(8,128)(2,1)}, u32[]{:S(2)}, u32[]{:S(2)}) %collective-permute-start) | collective-permute-done | bytes 524320 | tf_op jit(solution)/shard_map/while/body/eval_jaxpr/ppermute | solution.py:17
  339.0 3.5 fusion.157
  342.5 5.2 %collective-permute-start = (bf16[16,128,128]{2,1,0:T(8,128)(2,1)}, bf16[16,128,128]{2,1,0:T(8,128)(2,1)}, u32[]{:S(2)}, u32[]{:S(2)}) collective-permute-start(bf16[16,128,128]{2,1,0:T(8,128)(2,1)} %fusion.157), channel_id=1, source_target_pairs={{0,4},{4,8},{8,12},{1,5},{5,9},{9,13},{2,6},{6,10},{10,14},{3,7},{... | collective-permute-start | bytes 1572872 | tf_op jit(solution)/shard_map/while/body/eval_jaxpr/ppermute | solution.py:17
  347.7 9.2 %collective-permute-done = bf16[16,128,128]{2,1,0:T(8,128)(2,1)} collective-permute-done((bf16[16,128,128]{2,1,0:T(8,128)(2,1)}, bf16[16,128,128]{2,1,0:T(8,128)(2,1)}, u32[]{:S(2)}, u32[]{:S(2)}) %collective-permute-start) | collective-permute-done | bytes 524320 | tf_op jit(solution)/shard_map/while/body/eval_jaxpr/ppermute | solution.py:17
  358.0 3.5 fusion.157
  361.5 5.2 %collective-permute-start = (bf16[16,128,128]{2,1,0:T(8,128)(2,1)}, bf16[16,128,128]{2,1,0:T(8,128)(2,1)}, u32[]{:S(2)}, u32[]{:S(2)}) collective-permute-start(bf16[16,128,128]{2,1,0:T(8,128)(2,1)} %fusion.157), channel_id=1, source_target_pairs={{0,4},{4,8},{8,12},{1,5},{5,9},{9,13},{2,6},{6,10},{10,14},{3,7},{... | collective-permute-start | bytes 1572872 | tf_op jit(solution)/shard_map/while/body/eval_jaxpr/ppermute | solution.py:17
  366.7 8.3 %collective-permute-done = bf16[16,128,128]{2,1,0:T(8,128)(2,1)} collective-permute-done((bf16[16,128,128]{2,1,0:T(8,128)(2,1)}, bf16[16,128,128]{2,1,0:T(8,128)(2,1)}, u32[]{:S(2)}, u32[]{:S(2)}) %collective-permute-start) | collective-permute-done | bytes 524320 | tf_op jit(solution)/shard_map/while/body/eval_jaxpr/ppermute | solution.py:17
  376.3 2.4 convolution_subtract_fusion.5
  378.8 2.2 convolution_add_fusion.2
  383.2 2.2 convolution_select_fusion.2
  387.2 7.1 %reshape_squeeze.3 = bf16[3072,576]{1,0:T(8,128)(2,1)} reshape(bf16[1,192,9216]{2,1,0:T(8,128)(2,1)} %param.19) | data formatting | bytes 7077888 | tf_op jit(solution)/shard_map/reshape;squeeze | solution.py:161
  394.4 3.5 convolution_subtract_fusion.4
  397.9 2.6 convolution_add_fusion.1
  401.6 1.9 convolution_subtract_fusion.3
  403.5 3.0 convolution_select_fusion.1
  406.5 7.0 %select_reduce_fusion = (f32[3072]{0:T(1024)S(1)}, f32[3072,768]{0,1:T(8,128)S(1)}) fusion(s32[3072]{0:T(1024)S(1)} %eq.140, s32[3072]{0:T(1024)S(1)} %le.114, s32[768]{0:T(1024)S(1)} %convert_reduce_fusion, bf16[3072,576]{1,0:T(8,128)(2,1)} %reshape_squeeze.3, bf16[768,576]{1,0:T(8,128)(2,1)} %bitcast.36), kind=kOutput, calls=%fused_computation.7 | convolution fusion | flops 2732061696 | bytes 13900800 | tf_op jit(solution)/shard_map/dot_general | solution.py:184
  413.5 3.7 fusion.6
  417.2 5.6 %divide_convert_fusion = bf16[3072,512]{1,0:T(8,128)(2,1)S(1)} fusion(f32[3072]{0:T(1024)S(1)} %fusion.6, f32[3072,768]{0,1:T(8,128)S(1)} %get-tuple-element.87, f32[3072]{0:T(1024)S(1)} %broadcast_maximum_fusion, s32[3072]{0:T(1024)S(1)} %eq.140, s32[3072]{0:T(1024)S(1)} %le.114, s32[768]{0:T(1024)S(1)} %convert_reduce_fusion, bf16[768,576]{1,0:T(8,128)(2,1)} %bitcast.36), kind=kOutput, calls=%fused_computation.10 | convolution fusion | flops 2435579904 | bytes 13421568 | tf_op jit(solution)/shard_map/dot_general | solution.py:197
  422.9 3.7 fusion.20
  426.6 3.0 convolution_convert_fusion
  429.7 1.9 fusion.119
  431.6 2.4 convolution_select_fusion
  440.2 2.1 convert_element_type.184
  442.3 7.9 %reduce-scatter.2.cloned.1.call-done = bf16[96,2304]{1,0:T(8,128)(2,1)} async-done(((bf16[192,2304]{1,0:T(8,128)(2,1)}), bf16[96,2304]{1,0:T(8,128)(2,1)}) %reduce-scatter.2.cloned.1.call-update) | async-done | bytes 442384 | tf_op jit(solution)/shard_map/reduce_scatter | solution.py:208
  (158 shorter events, 38.3 us)
Async XLA Ops:
  7.2 415.7 %copy-start = (bf16[16,512,128]{2,1,0:T(8,128)(2,1)S(1)}, bf16[16,512,128]{2,1,0:T(8,128)(2,1)}, u32[]{:S(2)}) copy-start(bf16[16,512,128]{2,1,0:T(8,128)(2,1)} %param.21) | copy-start | bytes 6291460
  9.3 397.2 %all-to-all-start = ((bf16[4,1,192,576]{3,2,1,0:T(8,128)(2,1)}), bf16[4,1,192,576]{3,2,1,0:T(8,128)(2,1)}, u32[]{:S(2)}, u32[]{:S(2)}) async-start(bf16[4,1,192,576]{3,2,1,0:T(8,128)(2,1)} %stack.2), calls=%async_computation | async-start | bytes 1966080 | tf_op jit(solution)/shard_map/all_to_all | solution.py:169
  15.6 434.6 %reduce-scatter.2.cloned.1.call-start = ((), (), s32[]{:S(2)}) async-start(), calls=%async_computation.2 | async-start | bytes 1327104 | tf_op jit(solution)/shard_map/reduce_scatter | solution.py:208
  16.9 5.0 %copy-start.42 = (s32[1,8]{1,0:T(1,128)S(1)}, s32[1,8]{1,0:T(1,128)}, u32[]{:S(2)}) copy-start(s32[1,8]{1,0:T(1,128)} %param.23) | copy-start | bytes 100
  16.9 9.8 %copy-start.41 = (f32[1,16,192]{2,1,0:T(8,128)S(1)}, f32[1,16,192]{2,1,0:T(8,128)}, u32[]{:S(2)}) copy-start(f32[1,16,192]{2,1,0:T(8,128)} %param.18) | copy-start | bytes 36868
  17.2 2.1 copy-start.33
  29.7 1.2 copy-start.1
  114.5 1.6 copy-start.2
  114.6 1.7 copy-start.10
  118.9 1.5 copy-start.39
  121.5 5.3 %copy-start.29 = (f32[16,64,256]{2,1,0:T(8,128)}, f32[16,64,256]{2,1,0:T(8,128)S(1)}, u32[]{:S(2)}) copy-start(f32[16,64,256]{2,1,0:T(8,128)S(1)} %fusion.52) | copy-start | bytes 3145732
  123.4 5.4 %copy-start.24 = (f32[16,128,128]{2,1,0:T(8,128)}, f32[16,128,128]{2,1,0:T(8,128)S(1)}, u32[]{:S(2)}) copy-start(f32[16,128,128]{2,1,0:T(8,128)S(1)} %fusion.68) | copy-start | bytes 3145732
  126.8 4.0 copy-start.16
  212.9 2.6 copy-start.3
  212.9 2.6 copy-start.6
  215.5 6.0 %copy-start.28 = (f32[16,64,256]{2,1,0:T(8,128)}, f32[16,64,256]{2,1,0:T(8,128)S(1)}, u32[]{:S(2)}) copy-start(f32[16,64,256]{2,1,0:T(8,128)S(1)} %fusion.48) | copy-start | bytes 3145732
  218.4 3.1 copy-start.13
  305.4 3.2 copy-start.35
  305.4 3.2 copy-start.37
  305.4 3.2 copy-start.40
  308.5 1.4 copy-start.4
  308.5 1.5 copy-start.14
  309.6 3.6 copy-start.30
  313.3 2.9 copy-start.18
  313.3 2.9 copy-start.32
  323.0 14.8 %collective-permute-start = (bf16[16,128,128]{2,1,0:T(8,128)(2,1)}, bf16[16,128,128]{2,1,0:T(8,128)(2,1)}, u32[]{:S(2)}, u32[]{:S(2)}) collective-permute-start(bf16[16,128,128]{2,1,0:T(8,128)(2,1)} %fusion.157), channel_id=1, source_target_pairs={{0,4},{4,8},{8,12},{1,5},{5,9},{9,13},{2,6},{6,10},{10,14},{3,7},{... | collective-permute-start | bytes 1572872 | tf_op jit(solution)/shard_map/while/body/eval_jaxpr/ppermute | solution.py:17
  342.5 14.4 %collective-permute-start = (bf16[16,128,128]{2,1,0:T(8,128)(2,1)}, bf16[16,128,128]{2,1,0:T(8,128)(2,1)}, u32[]{:S(2)}, u32[]{:S(2)}) collective-permute-start(bf16[16,128,128]{2,1,0:T(8,128)(2,1)} %fusion.157), channel_id=1, source_target_pairs={{0,4},{4,8},{8,12},{1,5},{5,9},{9,13},{2,6},{6,10},{10,14},{3,7},{... | collective-permute-start | bytes 1572872 | tf_op jit(solution)/shard_map/while/body/eval_jaxpr/ppermute | solution.py:17
  361.5 13.5 %collective-permute-start = (bf16[16,128,128]{2,1,0:T(8,128)(2,1)}, bf16[16,128,128]{2,1,0:T(8,128)(2,1)}, u32[]{:S(2)}, u32[]{:S(2)}) collective-permute-start(bf16[16,128,128]{2,1,0:T(8,128)(2,1)} %fusion.157), channel_id=1, source_target_pairs={{0,4},{4,8},{8,12},{1,5},{5,9},{9,13},{2,6},{6,10},{10,14},{3,7},{... | collective-permute-start | bytes 1572872 | tf_op jit(solution)/shard_map/while/body/eval_jaxpr/ppermute | solution.py:17
  376.3 2.4 copy-start.17
  376.3 2.4 copy-start.25
  378.8 2.2 copy-start.38
  382.7 4.1 copy-start.22
  394.3 3.6 copy-start.19
  394.3 3.6 copy-start.20
  397.9 3.6 copy-start.31
  400.5 1.0 copy-start.26
  401.6 1.9 copy-start.7
  413.5 13.0 %slice-start = ((s8[9437184]{0:T(1024)(128)(4,1)}), s8[4194304]{0:T(1024)(128)(4,1)S(1)}, s32[]{:S(2)}) async-start(s8[9437184]{0:T(1024)(128)(4,1)} %bitcast.153), calls=%async_computation.3 | async-start | bytes 8388608
  417.2 9.4 %slice-start.1 = ((s8[9437184]{0:T(1024)(128)(4,1)}), s8[4194304]{0:T(1024)(128)(4,1)S(1)}, s32[]{:S(2)}) async-start(s8[9437184]{0:T(1024)(128)(4,1)} %bitcast.153), calls=%async_computation.4 | async-start | bytes 8388608
  417.2 9.4 %slice-start.2 = ((s8[9437184]{0:T(1024)(128)(4,1)}), s8[1048576]{0:T(1024)(128)(4,1)S(1)}, s32[]{:S(2)}) async-start(s8[9437184]{0:T(1024)(128)(4,1)} %bitcast.153), calls=%async_computation.5 | async-start | bytes 2097152
  429.6 1.9 copy-start.15
  431.6 2.5 copy-start.36
  431.6 3.4 copy-start.12
  431.6 3.4 copy-start.23
  431.6 3.4 copy-start.34
  435.0 1.1 copy-start.8
  435.0 1.4 copy-start.21
  436.4 1.2 copy-start.27
  (3 other events, 3.1 us)
Sparse Core Ops, SparseCore 0:
  429.8 20.4 reduce-scatter.1
